TPU v7x, 256 devices: a whole 4x4x8 slice. The times are simulated.
256 devices in a mesh: row: 8 (over y, x_hi), col: 32 (over x_lo, z, core).
Axes of the slice: x: 4 (x_hi: 2, x_lo: 2; x = x_hi * 2 + x_lo), y: 4, z: 8, core: 2. Of those that a mesh axis runs over, the one named last changes fastest.
Arguments:
- inverse_block: float32 [12288, 12288], P('row', 'col'), may hold values from -6 to 6
- factor_panel: float32 [3, 12288, 256], P(None, ('row', 'col')), may hold values from -0.0546875 to 0.0546875
- diag_inverse: float32 [3, 256, 256], P(None, 'row'), may hold values from -6 to 6
- block_lists: int32 [3, 48], replicated, may hold values from 0 to 47, as said below
- list_counts: int32 [3], replicated, may hold values from 6 to 48, as said below
Outputs:
- solved: float32 [3, 12288, 256], P(None, ('row', 'col'))
- diag_block: float32 [3, 256, 256], P(None, 'row')
Inputs may be any that keep to these rules, and one draw needn't show every extreme that they name: `block_lists`: row k is an ordering of all 48 ancestor blocks; its first list_counts[k] entries are the blocks listed for supernode k. `list_counts`: one supernode lists all 48 blocks and one lists 48 // 8 of them.
All inputs are finite; a program needn't handle non-finite values.
Results may differ from a plain program's by a relative error of at most 0.000071.
Values sent between devices are 32-bit elements; how exact they have to be, the bound alone decides.
No kernel may reach another device: no remote copies, remote signals or barrier semaphores. Data moves between devices by JAX's collectives and lax.ppermute only.
A program may use at most 64 MiB of HBM per device.

v0:
```python
import jax
import jax.numpy as jnp
from jax import lax
from jax.sharding import PartitionSpec as P

NA = 12288
BLK = 256
NSN = 3


def broadcast(block, axis, source):
    block = jnp.where(lax.axis_index(axis) == source, block, jnp.zeros_like(block))
    return lax.psum(block, axis)


def listed_table(block_lists, list_counts, nblocks):
    entries = jnp.arange(block_lists.shape[1], dtype=jnp.int32)
    active = entries[None, :] < list_counts[:, None]
    hits = (
        block_lists[:, :, None] == jnp.arange(nblocks, dtype=jnp.int32)[None, None, :]
    ) & active[:, :, None]
    return jnp.any(hits, axis=1).astype(jnp.float32)


def rows_mask(table, first_row, count):
    global_rows = first_row + jnp.arange(count, dtype=jnp.int32)
    onehot = (
        (global_rows // BLK)[:, None] == jnp.arange(table.shape[1], dtype=jnp.int32)[None, :]
    ).astype(jnp.float32)
    return jnp.dot(table, onehot.T, precision=lax.Precision.HIGHEST)


def apply_block(inverse_block, panels):
    panel_rows = panels[0]
    summed = jnp.dot(inverse_block, panel_rows, precision=lax.Precision.HIGHEST)
    results = [summed]
    return jnp.stack(results)


def per_device(inverse_block, factor_panel, diag_inverse, block_lists, list_counts):
    n_row = lax.axis_size("row")
    n_col = lax.axis_size("col")
    row_id = lax.axis_index("row")
    col_id = lax.axis_index("col")
    local_rows = factor_panel.shape[1]
    span_row = inverse_block.shape[0]
    span_col = inverse_block.shape[1]
    table = listed_table(block_lists, list_counts, NA // BLK)
    mask_local = rows_mask(table, (row_id * n_col + col_id) * local_rows, local_rows)
    mask_range = rows_mask(table, row_id * span_row, span_row)
    group_ratio = n_col // n_row
    source_row = col_id // group_ratio
    start_col = col_id % group_ratio * span_col
    solved_parts = []
    for member in range(NSN):
        gathered = lax.all_gather(factor_panel[member : member + 1], "col", axis=1, tiled=True)
        masked_range = gathered * mask_range[member : member + 1, :, None]
        piece = lax.dynamic_slice_in_dim(masked_range, start_col, span_col, 1)
        columns = broadcast(piece, "row", source_row)
        partial_value = (
            apply_block(inverse_block, columns) * mask_range[member : member + 1, :, None]
        )
        solved_parts.append(
            -lax.psum_scatter(partial_value, "col", scatter_dimension=1, tiled=True)
        )
    solved = jnp.concatenate(solved_parts, axis=0)
    masked_local = factor_panel * mask_local[:, :, None]
    terms = jnp.einsum("knw,knv->kwv", masked_local, solved, precision=lax.Precision.HIGHEST)
    shares = lax.psum_scatter(terms, "row", scatter_dimension=1, tiled=True)
    diag_block = diag_inverse - lax.psum(shares, "col")
    return (solved, diag_block)


def solution(mesh):
    placed = (P("row", "col"), P(None, ("row", "col"), None), P(None, "row", None), P(), P())
    return jax.shard_map(
        per_device,
        mesh=mesh,
        in_specs=placed,
        out_specs=(P(None, ("row", "col"), None), P(None, "row", None)),
        check_vma=False,
    )
```

profile of v0, /device:TPU:6, one launch (start us, length us, event | category | flops | bytes accessed | tf_op | source)
XLA Modules:
  0.0 864.0 jit_solution(14889107816256516591)
XLA Ops:
  7.2 0.0 copy-start
  7.2 0.0 all-gather.6.cloned.1.call-start
  7.2 1.7 fusion.21
  8.9 0.0 all-gather.6.cloned.1.call-update
  8.9 0.0 all-gather.4.cloned.1.call-start
  9.0 0.7 all-gather.4.cloned.1.call-update
  9.7 0.0 all-gather.8.cloned.1.call-start
  9.7 0.7 all-gather.8.cloned.1.call-update
  10.4 0.0 all-reduce.13.cloned.1.call-start
  10.5 0.7 iota_compare_fusion.5
  11.2 0.8 fusion.15
  12.0 0.4 fusion.3
  12.4 0.1 slice_reduce_fusion.2
  12.5 0.1 dynamic-slice.7
  12.5 0.1 dynamic-slice.6
  12.6 0.1 dynamic-slice.8
  12.7 64.1 %all-gather.6.cloned.1.call-done = f32[1,1536,256]{2,1,0:T(8,128)} async-done(((f32[1,48,256]{2,1,0:T(8,128)}), f32[1,1536,256]{2,1,0:T(8,128)}) %all-gather.6.cloned.1.call-update) | async-done | bytes 1572880 | tf_op jit(solution)/shard_map/all_gather | solution.py:56
  76.8 1.9 fusion.7
  78.7 64.3 %all-gather.4.cloned.1.call-done = f32[1,1536,256]{2,1,0:T(8,128)} async-done(((f32[1,48,256]{2,1,0:T(8,128)}), f32[1,1536,256]{2,1,0:T(8,128)}) %all-gather.4.cloned.1.call-update) | async-done | bytes 1572880 | tf_op jit(solution)/shard_map/all_gather | solution.py:56
  143.0 1.9 fusion.9
  144.9 63.8 %all-gather.8.cloned.1.call-done = f32[1,1536,256]{2,1,0:T(8,128)} async-done(((f32[1,48,256]{2,1,0:T(8,128)}), f32[1,1536,256]{2,1,0:T(8,128)}) %all-gather.8.cloned.1.call-update) | async-done | bytes 1572880 | tf_op jit(solution)/shard_map/all_gather | solution.py:56
  208.7 1.9 fusion.5
  210.5 0.0 all-reduce.13.cloned.1.call-update
  210.6 0.0 all-reduce.11.cloned.1.call-start
  210.6 95.0 %all-reduce.13.cloned.1.call-done = (f32[384,256]{1,0:T(8,128)}, f32[384,256]{1,0:T(8,128)}, f32[384,256]{1,0:T(8,128)}) async-done(((f32[384,256]{1,0:T(8,128)}, f32[384,256]{1,0:T(8,128)}, f32[384,256]{1,0:T(8,128)}), (f32[384,256]{1,0:T(8,128)}, f32[384,256]{1,0:T(8,128)}, f32[384,256]{1,0:T(8,128)})) %all-reduce.13.cloned.1.call-update) | async-done | bytes 1179664 | tf_op jit(solution)/shard_map/psum | solution.py:13
  305.6 0.0 copy-done
  305.6 6.2 fusion
  311.7 0.0 copy-start.4
  311.7 4.9 copy.21
  316.6 0.0 copy-done.4
  316.6 5.2 fusion.1
  321.8 0.0 copy-start.3
  321.8 4.9 copy.23
  326.6 0.0 copy-done.3
  326.6 5.2 fusion.2
  331.8 4.8 copy.25
  336.7 0.0 copy-start.6
  336.7 0.0 copy-start.1
  336.7 0.0 all-reduce.11.cloned.1.call-update
  336.7 0.0 copy-start.5
  336.7 0.0 reduce-scatter.2.cloned.1.call-start
  336.8 0.6 copy-done.6
  337.3 0.6 dynamic-slice
  338.6 0.2 fusion.16
  338.8 235.7 %all-reduce.11.cloned.1.call-done = (f32[1,1536,256]{2,0,1:T(1,128)}, f32[1,1536,256]{2,0,1:T(1,128)}, f32[1,1536,256]{2,0,1:T(1,128)}) async-done(((f32[1,1536,256]{2,0,1:T(1,128)}, f32[1,1536,256]{2,0,1:T(1,128)}, f32[1,1536,256]{2,0,1:T(1,128)}), (f32[1,1536,256]{2,0,1:T(1,128)}, f32[1,1536,256]{2,0,1:T(1,128)}, f32[1,1536,256]{2,0,1:T(1,128)})) %all-reduce.11.cloned.1.call-update) | async-done | bytes 4718608
  574.4 0.8 constant_dynamic-slice_fusion
  575.3 0.8 constant_dynamic-slice_fusion.2
  576.1 0.0 copy-done.1
  576.1 0.0 copy-start.2
  576.1 1.8 fusion.11
  578.0 0.0 reduce-scatter.2.cloned.1.call-update
  578.0 0.0 all-reduce.9.cloned.1.call-start
  578.1 76.2 %reduce-scatter.2.cloned.1.call-done = f32[3,32,256]{2,1,0:T(8,128)} async-done(((f32[3,256,256]{2,1,0:T(8,128)}), f32[3,32,256]{2,1,0:T(8,128)}) %reduce-scatter.2.cloned.1.call-update) | async-done | bytes 98320 | tf_op jit(solution)/shard_map/reduce_scatter | solution.py:69
  654.2 0.0 all-reduce.9.cloned.1.call-update
  654.3 201.3 %all-reduce.9.cloned.1.call-done = f32[3,32,256]{2,1,0:T(8,128)} async-done(((f32[3,32,256]{2,1,0:T(8,128)}), f32[3,32,256]{2,1,0:T(8,128)}) %all-reduce.9.cloned.1.call-update) | async-done | bytes 98320 | tf_op jit(solution)/shard_map/psum | solution.py:70
  855.6 0.0 copy-done.5
  855.6 1.5 sub.22
  857.1 0.0 copy-done.2
  (6 shorter events, 0.1 us)
Async XLA Ops:
  7.2 298.4 %copy-start = (f32[1536,384]{1,0:T(8,128)S(1)}, f32[1536,384]{1,0:T(8,128)}, u32[]{:S(2)}) copy-start(f32[1536,384]{1,0:T(8,128)} %param.5) | copy-start | bytes 7077892
  7.2 69.6 %all-gather.6.cloned.1.call-start = ((), (), s32[]{:S(2)}) async-start(), calls=%async_computation.2 | async-start | bytes 1622016 | tf_op jit(solution)/shard_map/all_gather | solution.py:56
  8.9 134.1 %all-gather.4.cloned.1.call-start = ((), (), s32[]{:S(2)}) async-start(), calls=%async_computation.1 | async-start | bytes 1622016 | tf_op jit(solution)/shard_map/all_gather | solution.py:56
  9.7 199.0 %all-gather.8.cloned.1.call-start = ((), (), s32[]{:S(2)}) async-start(), calls=%async_computation.3 | async-start | bytes 1622016 | tf_op jit(solution)/shard_map/all_gather | solution.py:56
  10.4 295.2 %all-reduce.13.cloned.1.call-start = ((), (), s32[]{:S(2)}) async-start(), calls=%async_computation.7 | async-start | bytes 2359296 | tf_op jit(solution)/shard_map/psum | solution.py:13
  210.6 363.9 %all-reduce.11.cloned.1.call-start = ((), (), s32[]{:S(2)}) async-start(), calls=%async_computation.6 | async-start | bytes 9437184
  311.7 4.9 copy-start.4
  321.8 4.9 copy-start.3
  336.7 0.7 copy-start.6
  336.7 239.5 %copy-start.1 = (f32[3,48,256]{2,1,0:T(8,128)S(1)}, f32[3,48,256]{2,1,0:T(8,128)}, u32[]{:S(2)}) copy-start(f32[3,48,256]{2,1,0:T(8,128)} %param.6) | copy-start | bytes 442372
  336.7 518.9 %copy-start.5 = (f32[3,32,256]{2,1,0:T(8,128)S(1)}, f32[3,32,256]{2,1,0:T(8,128)}, u32[]{:S(2)}) copy-start(f32[3,32,256]{2,1,0:T(8,128)} %param.7) | copy-start | bytes 294916
  336.7 317.5 %reduce-scatter.2.cloned.1.call-start = ((), (), s32[]{:S(2)}) async-start(), calls=%async_computation.4 | async-start | bytes 884736 | tf_op jit(solution)/shard_map/reduce_scatter | solution.py:69
  576.1 281.0 %copy-start.2 = (f32[3,48,256]{2,1,0:T(8,128)}, f32[3,48,256]{2,1,0:T(8,128)S(1)}, u32[]{:S(2)}) copy-start(f32[3,48,256]{2,1,0:T(8,128)S(1)} %pad_maximum_fusion) | copy-start | bytes 442372
  578.0 277.5 %all-reduce.9.cloned.1.call-start = ((), (), s32[]{:S(2)}) async-start(), calls=%async_computation.5 | async-start | bytes 196608 | tf_op jit(solution)/shard_map/psum | solution.py:70
Sparse Core Ops, SparseCore 0:
  10.4 66.3 all-gather.5
  79.2 63.7 all-gather.3
  144.9 63.7 all-gather.7
  211.4 94.1 all-reduce.12
  336.8 237.5 all-reduce.10
  578.1 76.0 reduce-scatter.1
  656.9 198.6 all-reduce.8
where the time goes:
time: 865 us; the launch traced here: 864 us
  waiting for transfers between devices  802 us (93%)
  local copies, waits for them, and re-layouts  19.3 us (2%)
  matrix products  18.9 us (2%)
  between operations  14.9 us (2%)
  other arithmetic  8.73 us (1%)
    unnamed x8, waiting for transfers between devices  237 us
    psum x1, waiting for transfers between devices, per_device(): diag_block = diag_inverse - lax.psum(shares, 'col')  201 us
    all_gather x3, waiting for transfers between devices, per_device(): lax.all_gather(factor_panel[member:member + 1], 'col', axis=1, tiled=True)  192 us
    psum x1, waiting for transfers between devices, broadcast(): return lax.psum(block, axis)  95 us
    reduce_scatter x1, waiting for transfers between devices, per_device(): shares = lax.psum_scatter(terms, 'row', scatter_dimension=1, tiled=True)  76.2 us
  transfers between devices with their start and end apart: 7, of which 7 were waited for; matrix products, arithmetic and copies ran while one was open for 1% of the time, Pallas kernels for 0%

commit v1 on v0

--- a/solution.py
+++ b/solution.py
@@ -53,7 +53,9 @@
     start_col = col_id % group_ratio * span_col
     solved_parts = []
     for member in range(NSN):
-        gathered = lax.all_gather(factor_panel[member : member + 1], "col", axis=1, tiled=True)
+        block_2 = factor_panel[member : member + 1]
+        sent = jnp.stack([block_2] * lax.axis_size("col"))
+        gathered = jnp.concatenate(lax.all_to_all(sent, "col", 0, 0), axis=1)
         masked_range = gathered * mask_range[member : member + 1, :, None]
         piece = lax.dynamic_slice_in_dim(masked_range, start_col, span_col, 1)
         columns = broadcast(piece, "row", source_row)

time: 865 us -> 803 us (0.928)
  waiting for transfers between devices: 802 us -> 640 us
  blocking collectives: 0 us -> 94.4 us
    all_gather x3 -> x0, waiting for transfers between devices: 192 us -> none  [per_device(): lax.all_gather(factor_panel[member:member + 1], 'col', axis=1, tiled=True)]
    all_to_all x0 -> x2, blocking collectives: none -> 94.4 us  [per_device(): gathered = jnp.concatenate(lax.all_to_all(sent, 'col', 0, 0), axis=1)]
    all_to_all x0 -> x1, waiting for transfers between devices: none -> 33.1 us  [per_device(): gathered = jnp.concatenate(lax.all_to_all(sent, 'col', 0, 0), axis=1)]
    unnamed x8 -> x5, waiting for transfers between devices: 237 us -> 236 us
  transfers between devices with their start and end apart: 7 -> 5, of which waited for: 7 -> 5; matrix products, arithmetic and copies ran while one was open for 1% -> 1% of each run, Pallas kernels for 0% -> 0%
where the time goes in v1:
time: 803 us; the launch traced here: 802 us
  waiting for transfers between devices  640 us (80%)
  blocking collectives  94.4 us (12%)
  local copies, waits for them, and re-layouts  20.4 us (3%)
  matrix products  18.9 us (2%)
  between operations  14.6 us (2%)
    unnamed x5, waiting for transfers between devices  236 us
    psum x1, waiting for transfers between devices, per_device(): diag_block = diag_inverse - lax.psum(shares, 'col')  201 us
    all_to_all x2, blocking collectives, per_device(): gathered = jnp.concatenate(lax.all_to_all(sent, 'col', 0, 0), axis=1)  94.4 us
    psum x1, waiting for transfers between devices, broadcast(): return lax.psum(block, axis)  93.4 us
    reduce_scatter x1, waiting for transfers between devices, per_device(): shares = lax.psum_scatter(terms, 'row', scatter_dimension=1, tiled=True)  76.3 us
    all_to_all x1, waiting for transfers between devices, per_device(): gathered = jnp.concatenate(lax.all_to_all(sent, 'col', 0, 0), axis=1)  33.1 us
    dot_general x3, matrix products, apply_block(): summed = jnp.dot(inverse_block, panel_rows, precision=lax.Precision.HIGHEST)  16.5 us
  transfers between devices with their start and end apart: 5, of which 5 were waited for; matrix products, arithmetic and copies ran while one was open for 1% of the time, Pallas kernels for 0%

profile of v1, /device:TPU:6, one launch (start us, length us, event | category | flops | bytes accessed | tf_op | source)
XLA Modules:
  0.0 801.7 jit_solution(12433806089949368829)
XLA Ops:
  7.2 0.0 copy-start
  7.2 1.0 slice_bitcast_fusion.2
  8.2 0.2 stack.7
  8.4 49.8 %all_to_all.15 = f32[32,1,48,256]{3,2,1,0:T(8,128)} all-to-all(f32[32,1,48,256]{3,2,1,0:T(8,128)S(1)} %stack.7), channel_id=1, replica_groups=mesh['row'=8,'col'=32] {'col'}, dimensions={0} | all-to-all | bytes 3145728 | tf_op jit(solution)/shard_map/all_to_all | solution.py:58
  58.1 0.2 stack.6
  58.3 44.6 %all_to_all.16 = f32[32,1,48,256]{3,2,1,0:T(8,128)} all-to-all(f32[32,1,48,256]{3,2,1,0:T(8,128)S(1)} %stack.6), channel_id=1, replica_groups=mesh['row'=8,'col'=32] {'col'}, dimensions={0} | all-to-all | bytes 3145728 | tf_op jit(solution)/shard_map/all_to_all | solution.py:58
  102.9 1.3 stack.8
  104.3 0.0 copy-start.7
  104.3 0.0 copy-start.6
  104.3 6.1 all-to-all-start.2
  110.4 0.0 all-reduce.13.cloned.1.call-start
  110.5 0.0 copy-done.7
  110.5 0.1 iota_compare_fusion.5
  110.6 0.0 copy-done.6
  110.6 0.1 fusion.15
  110.7 0.4 fusion.3
  111.1 0.1 slice_reduce_fusion.2
  111.2 0.1 dynamic-slice.7
  111.2 0.1 dynamic-slice.6
  111.3 0.1 dynamic-slice.8
  111.4 1.9 fusion.7
  113.3 1.9 fusion.9
  115.1 33.1 %all-to-all-done.2 = f32[32,1,48,256]{3,2,1,0:T(8,128)} async-done(((f32[32,1,48,256]{3,2,1,0:T(8,128)}), f32[32,1,48,256]{3,2,1,0:T(8,128)}, u32[]{:S(2)}, u32[]{:S(2)}) %all-to-all-start.2) | async-done | bytes 1572896 | tf_op jit(solution)/shard_map/all_to_all | solution.py:58
  148.3 1.9 fusion.5
  150.1 0.0 all-reduce.13.cloned.1.call-update
  150.2 0.0 all-reduce.11.cloned.1.call-start
  150.2 93.4 %all-reduce.13.cloned.1.call-done = (f32[384,256]{1,0:T(8,128)}, f32[384,256]{1,0:T(8,128)}, f32[384,256]{1,0:T(8,128)}) async-done(((f32[384,256]{1,0:T(8,128)}, f32[384,256]{1,0:T(8,128)}, f32[384,256]{1,0:T(8,128)}), (f32[384,256]{1,0:T(8,128)}, f32[384,256]{1,0:T(8,128)}, f32[384,256]{1,0:T(8,128)})) %all-reduce.13.cloned.1.call-update) | async-done | bytes 1179664 | tf_op jit(solution)/shard_map/psum | solution.py:13
  243.6 0.0 copy-done
  243.6 6.2 fusion
  249.8 0.0 copy-start.4
  249.8 4.9 copy.21
  254.6 0.0 copy-done.4
  254.6 5.2 fusion.1
  259.8 0.0 copy-start.3
  259.8 4.9 copy.23
  264.7 0.0 copy-done.3
  264.7 5.2 fusion.2
  269.9 4.8 copy.25
  274.7 0.0 copy-start.8
  274.7 0.0 copy-start.1
  274.7 0.0 all-reduce.11.cloned.1.call-update
  274.7 0.0 copy-start.5
  274.8 0.0 reduce-scatter.2.cloned.1.call-start
  274.8 0.6 copy-done.8
  275.4 0.6 dynamic-slice
  276.6 0.2 fusion.16
  276.8 235.7 %all-reduce.11.cloned.1.call-done = (f32[1,1536,256]{2,0,1:T(1,128)}, f32[1,1536,256]{2,0,1:T(1,128)}, f32[1,1536,256]{2,0,1:T(1,128)}) async-done(((f32[1,1536,256]{2,0,1:T(1,128)}, f32[1,1536,256]{2,0,1:T(1,128)}, f32[1,1536,256]{2,0,1:T(1,128)}), (f32[1,1536,256]{2,0,1:T(1,128)}, f32[1,1536,256]{2,0,1:T(1,128)}, f32[1,1536,256]{2,0,1:T(1,128)})) %all-reduce.11.cloned.1.call-update) | async-done | bytes 4718608
  512.5 0.8 constant_dynamic-slice_fusion
  513.4 0.8 constant_dynamic-slice_fusion.2
  514.2 0.0 copy-done.1
  514.2 0.0 copy-start.2
  514.2 1.8 fusion.11
  516.1 0.0 reduce-scatter.2.cloned.1.call-update
  516.1 0.0 all-reduce.9.cloned.1.call-start
  516.2 76.3 %reduce-scatter.2.cloned.1.call-done = f32[3,32,256]{2,1,0:T(8,128)} async-done(((f32[3,256,256]{2,1,0:T(8,128)}), f32[3,32,256]{2,1,0:T(8,128)}) %reduce-scatter.2.cloned.1.call-update) | async-done | bytes 98320 | tf_op jit(solution)/shard_map/reduce_scatter | solution.py:71
  592.5 0.0 all-reduce.9.cloned.1.call-update
  592.5 201.1 %all-reduce.9.cloned.1.call-done = f32[3,32,256]{2,1,0:T(8,128)} async-done(((f32[3,32,256]{2,1,0:T(8,128)}), f32[3,32,256]{2,1,0:T(8,128)}) %all-reduce.9.cloned.1.call-update) | async-done | bytes 98320 | tf_op jit(solution)/shard_map/psum | solution.py:72
  793.6 0.0 copy-done.5
  793.6 1.5 sub.22
  795.2 0.0 copy-done.2
  (6 shorter events, 0.1 us)
Async XLA Ops:
  7.2 236.4 %copy-start = (f32[1536,384]{1,0:T(8,128)S(1)}, f32[1536,384]{1,0:T(8,128)}, u32[]{:S(2)}) copy-start(f32[1536,384]{1,0:T(8,128)} %param.5) | copy-start | bytes 7077892
  104.3 6.2 copy-start.7
  104.3 6.3 copy-start.6
  104.3 44.0 %all-to-all-start.2 = ((f32[32,1,48,256]{3,2,1,0:T(8,128)}), f32[32,1,48,256]{3,2,1,0:T(8,128)}, u32[]{:S(2)}, u32[]{:S(2)}) async-start(f32[32,1,48,256]{3,2,1,0:T(8,128)} %stack.8), calls=%async_computation.2 | async-start | bytes 3145728 | tf_op jit(solution)/shard_map/all_to_all | solution.py:58
  110.4 133.2 %all-reduce.13.cloned.1.call-start = ((), (), s32[]{:S(2)}) async-start(), calls=%async_computation.7 | async-start | bytes 2359296 | tf_op jit(solution)/shard_map/psum | solution.py:13
  150.2 362.4 %all-reduce.11.cloned.1.call-start = ((), (), s32[]{:S(2)}) async-start(), calls=%async_computation.6 | async-start | bytes 9437184
  249.8 4.9 copy-start.4
  259.8 4.9 copy-start.3
  274.7 0.7 copy-start.8
  274.7 239.5 %copy-start.1 = (f32[3,48,256]{2,1,0:T(8,128)S(1)}, f32[3,48,256]{2,1,0:T(8,128)}, u32[]{:S(2)}) copy-start(f32[3,48,256]{2,1,0:T(8,128)} %param.6) | copy-start | bytes 442372
  274.7 518.9 %copy-start.5 = (f32[3,32,256]{2,1,0:T(8,128)S(1)}, f32[3,32,256]{2,1,0:T(8,128)}, u32[]{:S(2)}) copy-start(f32[3,32,256]{2,1,0:T(8,128)} %param.7) | copy-start | bytes 294916
  274.8 317.7 %reduce-scatter.2.cloned.1.call-start = ((), (), s32[]{:S(2)}) async-start(), calls=%async_computation.4 | async-start | bytes 884736 | tf_op jit(solution)/shard_map/reduce_scatter | solution.py:71
  514.2 281.0 %copy-start.2 = (f32[3,48,256]{2,1,0:T(8,128)}, f32[3,48,256]{2,1,0:T(8,128)S(1)}, u32[]{:S(2)}) copy-start(f32[3,48,256]{2,1,0:T(8,128)S(1)} %pad_maximum_fusion) | copy-start | bytes 442372
  516.1 277.5 %all-reduce.9.cloned.1.call-start = ((), (), s32[]{:S(2)}) async-start(), calls=%async_computation.5 | async-start | bytes 196608 | tf_op jit(solution)/shard_map/psum | solution.py:72
Sparse Core Ops, SparseCore 0:
  150.3 93.2 all-reduce.12
  274.9 237.6 all-reduce.10
  516.4 76.0 reduce-scatter.1
  595.0 198.6 all-reduce.8
